TPU v7x, 128 devices: a whole 4x4x4 slice. The times are simulated.
128 devices in a mesh: segment: 8 (over z_hi, y), patch: 16 (over x, z_lo, core).
Axes of the slice: x: 4, y: 4, z: 4 (z_hi: 2, z_lo: 2; z = z_hi * 2 + z_lo), core: 2. Of those that a mesh axis runs over, the one named last changes fastest.
Arguments:
- features: bfloat16 [8, 2, 320, 64, 128], P('segment', None, None, 'patch'), may hold values from -48 to 48, as said below
- latent: float32 [2, 4, 64, 128], P(None, None, 'patch'), may hold values from -48 to 48
- plan_pos: int32 [2], replicated, may hold values from 0 to 9
- blocks_used: int32 [8], P('segment'), may hold values from 1 to 2, as said below
- conv1_w: bfloat16 [8, 2, 9, 320, 320], P('segment'), may hold values from -0.109375 to 0.109375
- conv2_w: bfloat16 [8, 2, 9, 320, 320], P('segment'), may hold values from -0.109375 to 0.109375
- norm_gain: float32 [8, 2, 2, 320], P('segment'), may hold values from 0.25 to 1.75
- norm_shift: float32 [8, 2, 2, 320], P('segment'), may hold values from -3 to 3
- in_w: bfloat16 [9, 320, 4], replicated, may hold values from -1 to 1
- head_w: bfloat16 [9, 4, 320], replicated, may hold values from -0.109375 to 0.109375
- head_gain: float32 [320], replicated, may hold values from 0.25 to 1.75
- head_shift: float32 [320], replicated, may hold values from -3 to 3
Outputs:
- latent_out: float32 [2, 4, 64, 128], P(None, None, 'patch', 'segment')
- features_out: bfloat16 [8, 2, 320, 64, 128], P('segment', None, None, 'patch')
Inputs may be any that keep to these rules, and one draw needn't show every extreme that they name: `features`: every entry lies within the range; row magnitudes vary over the rows. `blocks_used`: each section holds 1 or 2 blocks; both counts occur.
All inputs are finite; a program needn't handle non-finite values.
Results may differ from a plain program's by a relative error of at most 0.0075.
Values may be sent and summed in bfloat16 or wider, within the bound.
A program may use at most 64 MiB of HBM per device.

v0:
```python
import jax
import jax.numpy as jnp
from jax import lax
from jax.sharding import PartitionSpec as P

GROUPS = 32
STEPS = 2
SCHED = 12
epsilon = 1e-05
sigma_top = 3.0
sigma_low = 0.1
rho_power = 7.0


def with_halo(block, sides, width):
    for axis, dim in sides:
        count = lax.axis_size(axis)
        forward = [(i, i + 1) for i in range(count - 1)]
        backward = [(target, source) for source, target in forward]
        low = lax.ppermute(
            lax.slice_in_dim(block, block.shape[dim] - width, None, axis=dim), axis, forward
        )
        high = lax.ppermute(lax.slice_in_dim(block, 0, width, axis=dim), axis, backward)
        block = jnp.concatenate([low, block, high], axis=dim)
    return block


def from_behind(shard, axis, by):
    devices = lax.axis_size(axis)
    pairs = [(i, i + by) for i in range(devices) if 0 <= i + by < devices]
    return lax.ppermute(shard, axis, pairs)


def broadcast(shard, axis, root):
    mine = lax.axis_index(axis) == root
    return lax.psum(jnp.where(mine, shard, jnp.zeros_like(shard)), axis)


def sigma_at(position):
    fraction = position.astype(jnp.float32) / (SCHED - 1)
    top_root = sigma_top ** (1.0 / rho_power)
    low_root = sigma_low ** (1.0 / rho_power)
    return (top_root + fraction * (low_root - top_root)) ** rho_power


def group_moments(values):
    batch_size, chan_count, height, col_count = values.shape
    grouped = values.reshape(batch_size, GROUPS, chan_count // GROUPS, height, col_count)
    cell_count = chan_count // GROUPS * height * col_count * lax.axis_size("patch")
    center = lax.psum(jnp.sum(grouped, axis=(2, 3, 4)), "patch") / cell_count
    deviation = grouped - center[:, :, None, None, None]
    spread = lax.psum(jnp.sum(jnp.square(deviation), axis=(2, 3, 4)), "patch") / cell_count
    return (center, jnp.sqrt(spread + epsilon))


def norm_silu(values, moments, gain, shift):
    center, root_spread = moments
    batch_size, chan_count, height, col_count = values.shape
    grouped = values.reshape(batch_size, GROUPS, chan_count // GROUPS, height, col_count)
    normed = (
        (grouped - center[:, :, None, None, None]) / root_spread[:, :, None, None, None]
    ).reshape(values.shape)
    normed = normed * gain[None, :, None, None] + shift[None, :, None, None]
    return jax.nn.silu(normed)


def conv_valid(rows_in, kernel):
    padded = jnp.pad(rows_in, ((0, 0), (0, 0), (0, 0), (1, 1)))
    height = rows_in.shape[2] - 2
    col_count = rows_in.shape[3]
    accum = jnp.zeros((rows_in.shape[0], kernel.shape[1], height, col_count), jnp.float32)
    for tap_no in range(9):
        row_off, col_off = (tap_no // 3, tap_no % 3)
        window = padded[:, :, row_off : row_off + height, col_off : col_off + col_count]
        accum = accum + jnp.einsum(
            "oi,bihw->bohw", kernel[tap_no], window, preferred_element_type=jnp.float32
        )
    return accum


def with_rows(values):
    return with_halo(values, (("patch", 2),), 1)


def resnet_unit(hidden, kern_one, kern_two, gain_pair, shift_pair):
    hidden_wide = hidden.astype(jnp.float32)
    first_act = norm_silu(
        hidden_wide, group_moments(hidden_wide), gain_pair[0], shift_pair[0]
    ).astype(jnp.bfloat16)
    middle = conv_valid(with_rows(first_act), kern_one)
    second = norm_silu(middle, group_moments(middle), gain_pair[1], shift_pair[1]).astype(
        jnp.bfloat16
    )
    result = conv_valid(with_rows(second), kern_two)
    return (hidden_wide + result).astype(jnp.bfloat16)


def head_noise(source, head_w, head_gain, head_shift):
    source_wide = source.astype(jnp.float32)
    head_input = norm_silu(source_wide, group_moments(source_wide), head_gain, head_shift).astype(
        jnp.bfloat16
    )
    return conv_valid(with_rows(head_input), head_w)


def per_device(
    features,
    latent,
    plan_pos,
    blocks_used,
    conv1_w,
    conv2_w,
    norm_gain,
    norm_shift,
    in_w,
    head_w,
    head_gain,
    head_shift,
):
    segment_count = lax.axis_size("segment")
    segment_pos = lax.axis_index("segment")
    current = features[0]
    for step_no in range(STEPS):
        arrived = from_behind(current, "segment", 1)
        noise_local = head_noise(current, head_w, head_gain, head_shift)
        noise_pred = broadcast(noise_local, "segment", segment_count - 1)
        position = plan_pos + step_no
        sigma_now = sigma_at(position)
        sigma_next = sigma_at(position + 1)
        latent = latent + (sigma_next - sigma_now)[:, None, None, None] * noise_pred
        scaled = (latent / jnp.sqrt(sigma_next * sigma_next + 1.0)[:, None, None, None]).astype(
            jnp.bfloat16
        )
        entry_rows = conv_valid(with_rows(scaled), in_w).astype(jnp.bfloat16)
        source = jnp.where(segment_pos == 0, entry_rows, arrived)
        after_one = resnet_unit(
            source, conv1_w[0, 0], conv2_w[0, 0], norm_gain[0, 0], norm_shift[0, 0]
        )
        after_two = resnet_unit(
            after_one, conv1_w[0, 1], conv2_w[0, 1], norm_gain[0, 1], norm_shift[0, 1]
        )
        current = jnp.where(blocks_used[0] >= 2, after_two, after_one)
    col_share = latent.shape[3] // segment_count
    latent_part = lax.dynamic_slice_in_dim(latent, segment_pos * col_share, col_share, 3)
    return (latent_part, current[None])


def solution(mesh):
    placed = (
        P("segment", None, None, "patch", None),
        P(None, None, "patch", None),
        P(),
        P("segment"),
        P("segment", None, None, None, None),
        P("segment", None, None, None, None),
        P("segment", None, None, None),
        P("segment", None, None, None),
        P(),
        P(),
        P(),
        P(),
    )
    return jax.shard_map(
        per_device,
        mesh=mesh,
        in_specs=placed,
        out_specs=(P(None, None, "patch", "segment"), P("segment", None, None, "patch", None)),
        check_vma=False,
    )
```

profile of v0, /device:TPU:65, one launch (start us, length us, event | category | flops | bytes accessed | tf_op | source)
XLA Modules:
  0.0 886.7 jit_solution(16695528666948445930)
XLA Ops:
  0.7 2.4 convert_reduce_fusion.5
  3.2 27.2 %psum.154 = f32[2,32]{1,0:T(2,128)S(1)} all-reduce(f32[2,32]{1,0:T(2,128)S(1)} %reduce_sum.235), channel_id=1, replica_groups=mesh['segment'=8,'patch'=16] {'patch'}, use_global_device_ids=true, to_apply=%region_2.0 | all-reduce | flops 64 | bytes 512 | tf_op jit(solution)/shard_map/psum | solution.py:50
  30.7 8.3 fusion.81
  39.2 30.3 %psum.155 = f32[2,32]{1,0:T(2,128)S(1)} all-reduce(f32[2,32]{1,0:T(2,128)S(1)} %reduce_sum.241), channel_id=1, replica_groups=mesh['segment'=8,'patch'=16] {'patch'}, use_global_device_ids=true, to_apply=%region_5.6 | all-reduce | flops 64 | bytes 512 | tf_op jit(solution)/shard_map/psum | solution.py:52
  71.1 1.9 collective-permute-start
  73.1 3.2 collective-permute-start.1
  76.3 3.2 collective-permute-start.4
  79.5 2.6 fusion.135
  82.4 1.9 select_maximum_fusion.18
  87.4 33.3 %psum.156 = f32[2,4,4,128]{3,1,2,0:T(4,128)S(1)} all-reduce(f32[2,4,4,128]{3,1,2,0:T(4,128)S(1)} %fusion.115), channel_id=1, replica_groups=mesh['segment'=8,'patch'=16] {'segment'}, use_global_device_ids=true, to_apply=%region_6.7 | all-reduce | flops 4096 | bytes 32768 | tf_op jit(solution)/shard_map/psum | solution.py:36
  120.8 9.9 %collective-permute-start.2 = (bf16[2,4,1,128]{3,1,2,0:T(4,128)(2,1)S(1)}, bf16[2,4,1,128]{3,1,2,0:T(4,128)(2,1)S(1)}, u32[]{:S(2)}, u32[]{:S(2)}) collective-permute-start(bf16[2,4,1,128]{3,1,2,0:T(4,128)(2,1)S(1)} %get-tuple-element.38), channel_id=1, source_target_pairs={{0,1},{1,2},{2,3},{3,4},{4,5},{5,6},{6,7},{7,8},{8,9},{9,10},{10,1... | collective-permute-start | bytes 6152 | tf_op jit(solution)/shard_map/ppermute | solution.py:20
  131.5 1.9 collective-permute-start.3
  133.8 2.6 collective-permute-done.3
  140.0 24.6 %psum.157 = f32[2,32]{1,0:T(2,128)S(1)} all-reduce(f32[2,32]{1,0:T(2,128)S(1)} %reduce_sum.247), channel_id=1, replica_groups=mesh['segment'=8,'patch'=16] {'patch'}, use_global_device_ids=true, to_apply=%region_9.10 | all-reduce | flops 64 | bytes 512 | tf_op jit(solution)/shard_map/psum | solution.py:50
  165.4 29.9 %psum.158 = f32[2,32]{1,0:T(2,128)S(1)} all-reduce(f32[2,32]{1,0:T(2,128)S(1)} %reduce_sum.250), channel_id=1, replica_groups=mesh['segment'=8,'patch'=16] {'patch'}, use_global_device_ids=true, to_apply=%region_12.13 | all-reduce | flops 64 | bytes 512 | tf_op jit(solution)/shard_map/psum | solution.py:52
  196.2 1.9 collective-permute-start.5
  198.1 2.4 collective-permute-start.6
  202.1 2.6 collective-permute-done.6
  218.2 23.6 %psum.159 = f32[2,32]{1,0:T(2,128)S(1)} all-reduce(f32[2,32]{1,0:T(2,128)S(1)} %reduce_sum.256), channel_id=1, replica_groups=mesh['segment'=8,'patch'=16] {'patch'}, use_global_device_ids=true, to_apply=%region_15.16 | all-reduce | flops 64 | bytes 512 | tf_op jit(solution)/shard_map/psum | solution.py:50
  242.5 30.5 %psum.160 = f32[2,32]{1,0:T(2,128)S(1)} all-reduce(f32[2,32]{1,0:T(2,128)S(1)} %reduce_sum.262), channel_id=1, replica_groups=mesh['segment'=8,'patch'=16] {'patch'}, use_global_device_ids=true, to_apply=%region_18.19 | all-reduce | flops 64 | bytes 512 | tf_op jit(solution)/shard_map/psum | solution.py:52
  273.9 1.9 collective-permute-start.7
  275.8 2.4 collective-permute-start.8
  279.8 2.6 collective-permute-done.8
  293.9 1.9 convert_reduce_fusion.2
  296.0 23.8 %psum.161 = f32[2,32]{1,0:T(2,128)S(1)} all-reduce(f32[2,32]{1,0:T(2,128)S(1)} %reduce_sum.265), channel_id=1, replica_groups=mesh['segment'=8,'patch'=16] {'patch'}, use_global_device_ids=true, to_apply=%region_21.22 | all-reduce | flops 64 | bytes 512 | tf_op jit(solution)/shard_map/psum | solution.py:50
  320.6 30.5 %psum.162 = f32[2,32]{1,0:T(2,128)S(1)} all-reduce(f32[2,32]{1,0:T(2,128)S(1)} %reduce_sum.271), channel_id=1, replica_groups=mesh['segment'=8,'patch'=16] {'patch'}, use_global_device_ids=true, to_apply=%region_24.25 | all-reduce | flops 64 | bytes 512 | tf_op jit(solution)/shard_map/psum | solution.py:52
  352.0 1.9 collective-permute-start.9
  353.9 2.4 collective-permute-start.10
  357.9 2.6 collective-permute-done.10
  374.0 23.6 %psum.163 = f32[2,32]{1,0:T(2,128)S(1)} all-reduce(f32[2,32]{1,0:T(2,128)S(1)} %reduce_sum.277), channel_id=1, replica_groups=mesh['segment'=8,'patch'=16] {'patch'}, use_global_device_ids=true, to_apply=%region_27.28 | all-reduce | flops 64 | bytes 512 | tf_op jit(solution)/shard_map/psum | solution.py:50
  398.3 30.5 %psum.164 = f32[2,32]{1,0:T(2,128)S(1)} all-reduce(f32[2,32]{1,0:T(2,128)S(1)} %reduce_sum.280), channel_id=1, replica_groups=mesh['segment'=8,'patch'=16] {'patch'}, use_global_device_ids=true, to_apply=%region_30.31 | all-reduce | flops 64 | bytes 512 | tf_op jit(solution)/shard_map/psum | solution.py:52
  429.7 1.9 collective-permute-start.11
  431.6 2.6 collective-permute-start.12
  435.7 2.5 collective-permute-done.12
  449.7 2.0 convert_reduce_fusion.4
  451.9 23.6 %psum.165 = f32[2,32]{1,0:T(2,128)S(1)} all-reduce(f32[2,32]{1,0:T(2,128)S(1)} %reduce_sum.286), channel_id=1, replica_groups=mesh['segment'=8,'patch'=16] {'patch'}, use_global_device_ids=true, to_apply=%region_33.34 | all-reduce | flops 64 | bytes 512 | tf_op jit(solution)/shard_map/psum | solution.py:50
  475.7 1.9 collective-permute-start.17
  478.2 30.8 %psum.166 = f32[2,32]{1,0:T(2,128)S(1)} all-reduce(f32[2,32]{1,0:T(2,128)S(1)} %reduce_sum.292), channel_id=1, replica_groups=mesh['segment'=8,'patch'=16] {'patch'}, use_global_device_ids=true, to_apply=%region_36.37 | all-reduce | flops 64 | bytes 512 | tf_op jit(solution)/shard_map/psum | solution.py:52
  509.8 1.9 collective-permute-start.13
  511.7 2.4 collective-permute-start.14
  515.7 2.6 collective-permute-done.14
  521.5 34.6 %psum.167 = f32[2,4,4,128]{3,1,2,0:T(4,128)S(1)} all-reduce(f32[2,4,4,128]{3,1,2,0:T(4,128)S(1)} %fusion.107), channel_id=1, replica_groups=mesh['segment'=8,'patch'=16] {'segment'}, use_global_device_ids=true, to_apply=%region_37.38 | all-reduce | flops 4096 | bytes 32768 | tf_op jit(solution)/shard_map/psum | solution.py:36
  556.2 9.6 %collective-permute-start.15 = (bf16[2,4,1,128]{3,1,2,0:T(4,128)(2,1)S(1)}, bf16[2,4,1,128]{3,1,2,0:T(4,128)(2,1)S(1)}, u32[]{:S(2)}, u32[]{:S(2)}) collective-permute-start(bf16[2,4,1,128]{3,1,2,0:T(4,128)(2,1)S(1)} %get-tuple-element.36), channel_id=1, source_target_pairs={{0,1},{1,2},{2,3},{3,4},{4,5},{5,6},{6,7},{7,8},{8,9},{9,10},{10,1... | collective-permute-start | bytes 6152 | tf_op jit(solution)/shard_map/ppermute | solution.py:20
  565.8 2.3 collective-permute-start.16
  574.3 24.6 %psum.168 = f32[2,32]{1,0:T(2,128)S(1)} all-reduce(f32[2,32]{1,0:T(2,128)S(1)} %reduce_sum.295), channel_id=1, replica_groups=mesh['segment'=8,'patch'=16] {'patch'}, use_global_device_ids=true, to_apply=%region_40.41 | all-reduce | flops 64 | bytes 512 | tf_op jit(solution)/shard_map/psum | solution.py:50
  599.7 29.5 %psum.169 = f32[2,32]{1,0:T(2,128)S(1)} all-reduce(f32[2,32]{1,0:T(2,128)S(1)} %reduce_sum.361), channel_id=1, replica_groups=mesh['segment'=8,'patch'=16] {'patch'}, use_global_device_ids=true, to_apply=%region_43.44 | all-reduce | flops 64 | bytes 512 | tf_op jit(solution)/shard_map/psum | solution.py:52
  630.0 1.9 collective-permute-start.18
  631.9 2.4 collective-permute-start.19
  635.9 2.6 collective-permute-done.19
  651.9 23.6 %psum.170 = f32[2,32]{1,0:T(2,128)S(1)} all-reduce(f32[2,32]{1,0:T(2,128)S(1)} %reduce_sum.364), channel_id=1, replica_groups=mesh['segment'=8,'patch'=16] {'patch'}, use_global_device_ids=true, to_apply=%region_46.47 | all-reduce | flops 64 | bytes 512 | tf_op jit(solution)/shard_map/psum | solution.py:50
  676.3 30.5 %psum.171 = f32[2,32]{1,0:T(2,128)S(1)} all-reduce(f32[2,32]{1,0:T(2,128)S(1)} %reduce_sum.367), channel_id=1, replica_groups=mesh['segment'=8,'patch'=16] {'patch'}, use_global_device_ids=true, to_apply=%region_49.50 | all-reduce | flops 64 | bytes 512 | tf_op jit(solution)/shard_map/psum | solution.py:52
  707.6 1.9 collective-permute-start.20
  709.6 2.6 collective-permute-start.21
  713.6 2.6 collective-permute-done.21
  729.7 23.6 %psum.172 = f32[2,32]{1,0:T(2,128)S(1)} all-reduce(f32[2,32]{1,0:T(2,128)S(1)} %reduce_sum.370), channel_id=1, replica_groups=mesh['segment'=8,'patch'=16] {'patch'}, use_global_device_ids=true, to_apply=%region_52.53 | all-reduce | flops 64 | bytes 512 | tf_op jit(solution)/shard_map/psum | solution.py:50
  754.1 30.5 %psum.173 = f32[2,32]{1,0:T(2,128)S(1)} all-reduce(f32[2,32]{1,0:T(2,128)S(1)} %reduce_sum.373), channel_id=1, replica_groups=mesh['segment'=8,'patch'=16] {'patch'}, use_global_device_ids=true, to_apply=%region_55.56 | all-reduce | flops 64 | bytes 512 | tf_op jit(solution)/shard_map/psum | solution.py:52
  785.5 1.9 collective-permute-start.22
  787.4 2.4 collective-permute-start.23
  791.4 2.6 collective-permute-done.23
  807.4 23.6 %psum.174 = f32[2,32]{1,0:T(2,128)S(1)} all-reduce(f32[2,32]{1,0:T(2,128)S(1)} %reduce_sum.376), channel_id=1, replica_groups=mesh['segment'=8,'patch'=16] {'patch'}, use_global_device_ids=true, to_apply=%region_58.59 | all-reduce | flops 64 | bytes 512 | tf_op jit(solution)/shard_map/psum | solution.py:50
  831.8 30.7 %psum.175 = f32[2,32]{1,0:T(2,128)S(1)} all-reduce(f32[2,32]{1,0:T(2,128)S(1)} %reduce_sum.379), channel_id=1, replica_groups=mesh['segment'=8,'patch'=16] {'patch'}, use_global_device_ids=true, to_apply=%region_61.62 | all-reduce | flops 64 | bytes 512 | tf_op jit(solution)/shard_map/psum | solution.py:52
  863.3 1.9 collective-permute-start.24
  865.3 2.4 collective-permute-start.25
  869.3 2.6 collective-permute-done.25
  (290 shorter events, 151.4 us)
Async XLA Ops:
  0.6 69.1 %copy-start = (bf16[1,2,320,4,128]{4,3,2,1,0:T(4,128)(2,1)S(1)}, bf16[1,2,320,4,128]{4,3,2,1,0:T(4,128)(2,1)}, u32[]{:S(2)}) copy-start(bf16[1,2,320,4,128]{4,3,2,1,0:T(4,128)(2,1)} %param.12) | copy-start | bytes 1966084
  0.6 69.1 %copy-start.4 = (f32[320]{0:T(512)S(1)}, f32[320]{0:T(512)}, u32[]{:S(2)}) copy-start(f32[320]{0:T(512)} %param.22) | copy-start | bytes 3844
  0.7 69.1 %copy-start.3 = (f32[320]{0:T(512)S(1)}, f32[320]{0:T(512)}, u32[]{:S(2)}) copy-start(f32[320]{0:T(512)} %param.23) | copy-start | bytes 3844
  71.1 11.3 %collective-permute-start = (bf16[2,320,1,128]{3,1,2,0:T(8,128)(2,1)}, bf16[2,320,1,128]{3,1,2,0:T(8,128)(2,1)}, u32[]{:S(2)}, u32[]{:S(2)}) collective-permute-start(bf16[2,320,1,128]{3,1,2,0:T(8,128)(2,1)} %get-tuple-element.34), channel_id=1, source_target_pairs={{0,1},{1,2},{2,3},{3,4},{4,5},{5,6},{6,7},{7,8},{8,9},{9,10},{10,1... | collective-permute-start | bytes 491528 | tf_op jit(solution)/shard_map/ppermute | solution.py:20
  73.0 9.1 %copy-start.8 = (bf16[9,4,320]{2,1,0:T(4,128)(2,1)S(1)}, bf16[9,4,320]{2,1,0:T(4,128)(2,1)}, u32[]{:S(2)}) copy-start(bf16[9,4,320]{2,1,0:T(4,128)(2,1)} %param.21) | copy-start | bytes 69124
  73.1 9.3 %collective-permute-start.1 = (bf16[2,320,1,128]{3,1,2,0:T(8,128)(2,1)}, bf16[2,320,1,128]{3,1,2,0:T(8,128)(2,1)S(1)}, u32[]{:S(2)}, u32[]{:S(2)}) collective-permute-start(bf16[2,320,1,128]{3,1,2,0:T(8,128)(2,1)} %get-tuple-element.35), channel_id=1, source_target_pairs={{1,0},{2,1},{3,2},{4,3},{5,4},{6,5},{7,6},{8,7},{9,8},{10,9},{11,1... | collective-permute-start | bytes 491528 | tf_op jit(solution)/shard_map/ppermute | solution.py:23
  76.3 6.0 copy-start.7
  76.3 62.8 %collective-permute-start.4 = (bf16[2,320,4,128]{3,1,2,0:T(8,128)(2,1)S(1)}, bf16[2,320,4,128]{3,1,2,0:T(8,128)(2,1)S(1)}, u32[]{:S(2)}, u32[]{:S(2)}) collective-permute-start(bf16[2,320,4,128]{3,1,2,0:T(8,128)(2,1)S(1)} %bitcast.575), channel_id=1, source_target_pairs={{0,16},{16,32},{32,48},{48,64},{64,80},{80,96},{96,112},{1,17},{17... | collective-permute-start | bytes 1966088 | tf_op jit(solution)/shard_map/ppermute | solution.py:31
  86.8 34.0 %copy-start.2 = (f32[2,4,4,128]{3,2,1,0:T(4,128)S(1)}, f32[2,4,4,128]{3,2,1,0:T(4,128)}, u32[]{:S(2)}) copy-start(f32[2,4,4,128]{3,2,1,0:T(4,128)} %param.13) | copy-start | bytes 49156
  86.8 44.0 %copy-start.5 = (f32[1,2,2,320]{3,2,1,0:T(2,128)S(1)}, f32[1,2,2,320]{3,2,1,0:T(2,128)}, u32[]{:S(2)}) copy-start(f32[1,2,2,320]{3,2,1,0:T(2,128)} %param.19) | copy-start | bytes 15364
  86.8 44.0 %copy-start.6 = (f32[1,2,2,320]{3,2,1,0:T(2,128)S(1)}, f32[1,2,2,320]{3,2,1,0:T(2,128)}, u32[]{:S(2)}) copy-start(f32[1,2,2,320]{3,2,1,0:T(2,128)} %param.18) | copy-start | bytes 15364
  86.8 46.6 %copy-start.1 = (bf16[9,320,4]{1,2,0:T(4,128)(2,1)S(1)}, bf16[9,320,4]{1,2,0:T(4,128)(2,1)}, u32[]{:S(2)}) copy-start(bf16[9,320,4]{1,2,0:T(4,128)(2,1)} %param.20) | copy-start | bytes 69124
  120.8 12.6 %collective-permute-start.2 = (bf16[2,4,1,128]{3,1,2,0:T(4,128)(2,1)S(1)}, bf16[2,4,1,128]{3,1,2,0:T(4,128)(2,1)S(1)}, u32[]{:S(2)}, u32[]{:S(2)}) collective-permute-start(bf16[2,4,1,128]{3,1,2,0:T(4,128)(2,1)S(1)} %get-tuple-element.38), channel_id=1, source_target_pairs={{0,1},{1,2},{2,3},{3,4},{4,5},{5,6},{6,7},{7,8},{8,9},{9,10},{10,1... | collective-permute-start | bytes 6152 | tf_op jit(solution)/shard_map/ppermute | solution.py:20
  131.5 4.9 collective-permute-start.3
  196.2 5.9 collective-permute-start.5
  198.1 6.6 collective-permute-start.6
  273.9 5.9 collective-permute-start.7
  275.8 6.6 collective-permute-start.8
  352.0 5.9 collective-permute-start.9
  353.9 6.6 collective-permute-start.10
  429.7 6.0 collective-permute-start.11
  431.6 6.6 collective-permute-start.12
  475.7 97.7 %collective-permute-start.17 = (bf16[2,320,4,128]{3,1,2,0:T(8,128)(2,1)S(1)}, bf16[2,320,4,128]{3,1,2,0:T(8,128)(2,1)S(1)}, u32[]{:S(2)}, u32[]{:S(2)}) collective-permute-start(bf16[2,320,4,128]{3,1,2,0:T(8,128)(2,1)S(1)} %get-tuple-element.53), channel_id=1, source_target_pairs={{0,16},{16,32},{32,48},{48,64},{64,80},{80,96},{96,112},{1,17},{17... | collective-permute-start | bytes 1966088 | tf_op jit(solution)/shard_map/ppermute | solution.py:31
  509.8 5.9 collective-permute-start.13
  511.7 6.6 collective-permute-start.14
  556.2 12.6 %collective-permute-start.15 = (bf16[2,4,1,128]{3,1,2,0:T(4,128)(2,1)S(1)}, bf16[2,4,1,128]{3,1,2,0:T(4,128)(2,1)S(1)}, u32[]{:S(2)}, u32[]{:S(2)}) collective-permute-start(bf16[2,4,1,128]{3,1,2,0:T(4,128)(2,1)S(1)} %get-tuple-element.36), channel_id=1, source_target_pairs={{0,1},{1,2},{2,3},{3,4},{4,5},{5,6},{6,7},{7,8},{8,9},{9,10},{10,1... | collective-permute-start | bytes 6152 | tf_op jit(solution)/shard_map/ppermute | solution.py:20
  565.8 4.9 collective-permute-start.16
  630.0 5.9 collective-permute-start.18
  631.9 6.6 collective-permute-start.19
  707.6 6.0 collective-permute-start.20
  709.6 6.6 collective-permute-start.21
  785.5 5.9 collective-permute-start.22
  787.4 6.6 collective-permute-start.23
  863.3 5.9 collective-permute-start.24
  865.3 6.6 collective-permute-start.25
where the time goes:
time: 898 us; the launch traced here: 887 us
  blocking collectives  614 us (68%)
  matrix products  122 us (14%)
  starting transfers between devices  73.3 us (8%)
  other arithmetic  35.6 us (4%)
  waiting for transfers between devices  29.8 us (3%)
  local copies, waits for them, and re-layouts  9.08 us (1%)
    psum x10, blocking collectives, group_moments(): lax.psum(jnp.sum(jnp.square(deviation), axis=(2, 3, 4)), 'patch')  304 us
    psum x10, blocking collectives, group_moments(): center = lax.psum(jnp.sum(grouped, axis=(2, 3, 4)), 'patch') / cell_count  242 us
    dot_general x108, matrix products, conv_valid(): jnp.einsum('oi,bihw->bohw', kernel[tap_no], window, preferred_element_typ...  122 us
    psum x2, blocking collectives, broadcast(): return lax.psum(jnp.where(mine, shard, jnp.zeros_like(shard)), axis)  67.9 us
    ppermute x12, starting transfers between devices, with_halo(): lax.ppermute(lax.slice_in_dim(block, block.shape[dim] - width, None, axis...  38.7 us
    ppermute x12, starting transfers between devices, with_halo(): lax.ppermute(lax.slice_in_dim(block, 0, width, axis=dim), axis, backward)  29.5 us
    ppermute x12, waiting for transfers between devices, with_halo(): lax.ppermute(lax.slice_in_dim(block, 0, width, axis=dim), axis, backward)  27.7 us
  transfers between devices with their start and end apart: 26, of which 18 were waited for; matrix products, arithmetic and copies ran while one was open for 4% of the time, Pallas kernels for 0%

commit v1 on v0

--- a/solution.py
+++ b/solution.py
@@ -47,7 +47,7 @@
     batch_size, chan_count, height, col_count = values.shape
     grouped = values.reshape(batch_size, GROUPS, chan_count // GROUPS, height, col_count)
     cell_count = chan_count // GROUPS * height * col_count * lax.axis_size("patch")
-    center = lax.psum(jnp.sum(grouped, axis=(2, 3, 4)), "patch") / cell_count
+    center = jnp.sum(lax.all_gather(jnp.sum(grouped, axis=(2, 3, 4)), "patch"), axis=0) / cell_count
     deviation = grouped - center[:, :, None, None, None]
     spread = lax.psum(jnp.sum(jnp.square(deviation), axis=(2, 3, 4)), "patch") / cell_count
     return (center, jnp.sqrt(spread + epsilon))

time: 898 us -> 788 us (0.88)
  blocking collectives: 614 us -> 503 us
    psum x10 -> x0, blocking collectives: 242 us -> none  [group_moments(): center = lax.psum(jnp.sum(grouped, axis=(2, 3, 4)), 'patch') / cell_count]
    all_gather x0 -> x10, blocking collectives: none -> 167 us  [group_moments(): lax.all_gather(jnp.sum(grouped, axis=(2, 3, 4)), 'patch')]
    psum x10, blocking collectives: 304 us -> 268 us  [group_moments(): lax.psum(jnp.sum(jnp.square(deviation), axis=(2, 3, 4)), 'patch')]
where the time goes in v1:
time: 788 us; the launch traced here: 776 us
  blocking collectives  503 us (64%)
  matrix products  122 us (15%)
  starting transfers between devices  73.2 us (9%)
  other arithmetic  35.9 us (5%)
  waiting for transfers between devices  29.9 us (4%)
  local copies, waits for them, and re-layouts  9.08 us (1%)
    psum x10, blocking collectives, group_moments(): lax.psum(jnp.sum(jnp.square(deviation), axis=(2, 3, 4)), 'patch')  268 us
    all_gather x10, blocking collectives, group_moments(): lax.all_gather(jnp.sum(grouped, axis=(2, 3, 4)), 'patch')  167 us
    dot_general x108, matrix products, conv_valid(): jnp.einsum('oi,bihw->bohw', kernel[tap_no], window, preferred_element_typ...  122 us
    psum x2, blocking collectives, broadcast(): return lax.psum(jnp.where(mine, shard, jnp.zeros_like(shard)), axis)  67.7 us
    ppermute x12, starting transfers between devices, with_halo(): lax.ppermute(lax.slice_in_dim(block, block.shape[dim] - width, None, axis...  38.6 us
    ppermute x12, starting transfers between devices, with_halo(): lax.ppermute(lax.slice_in_dim(block, 0, width, axis=dim), axis, backward)  29.5 us
    ppermute x12, waiting for transfers between devices, with_halo(): lax.ppermute(lax.slice_in_dim(block, 0, width, axis=dim), axis, backward)  27.7 us
  transfers between devices with their start and end apart: 26, of which 18 were waited for; matrix products, arithmetic and copies ran while one was open for 4% of the time, Pallas kernels for 0%

profile of v1, /device:TPU:65, one launch (start us, length us, event | category | flops | bytes accessed | tf_op | source)
XLA Modules:
  0.0 776.0 jit_solution(15318753480237743719)
XLA Ops:
  0.7 2.4 convert_reduce_fusion.5
  3.2 20.2 %all-gather.10 = f32[16,2,32]{2,1,0:T(2,128)S(1)} all-gather(f32[1,2,32]{2,1,0:T(2,128)S(1)} %bitcast.586), channel_id=2, replica_groups=mesh['segment'=8,'patch'=16] {'patch'}, dimensions={0}, use_global_device_ids=true | all-gather | bytes 4352 | tf_op jit(solution)/shard_map/all_gather | solution.py:50
  23.7 8.3 %fusion.81 = f32[2,320]{1,0:T(2,128)S(1)} fusion(bf16[1,2,320,4,128]{4,3,2,1,0:T(4,128)(2,1)} %param.12, f32[2,320]{1,0:T(2,128)S(1)} %sub.193), kind=kLoop, calls=%fused_computation.150 | loop fusion | flops 1310080 | bytes 660480 | tf_op jit(solution)/shard_map/reduce_sum | solution.py:52
  32.2 26.7 %psum.84 = f32[2,32]{1,0:T(2,128)S(1)} all-reduce(f32[2,32]{1,0:T(2,128)S(1)} %reduce_sum.328), channel_id=1, replica_groups=mesh['segment'=8,'patch'=16] {'patch'}, use_global_device_ids=true, to_apply=%region_5.6 | all-reduce | flops 64 | bytes 512 | tf_op jit(solution)/shard_map/psum | solution.py:52
  60.5 1.9 collective-permute-start
  62.5 3.2 collective-permute-start.1
  65.7 3.2 collective-permute-start.4
  69.0 2.6 fusion.135
  71.8 1.9 select_maximum_fusion.18
  76.8 33.3 %psum.85 = f32[2,4,4,128]{3,1,2,0:T(4,128)S(1)} all-reduce(f32[2,4,4,128]{3,1,2,0:T(4,128)S(1)} %fusion.115), channel_id=1, replica_groups=mesh['segment'=8,'patch'=16] {'segment'}, use_global_device_ids=true, to_apply=%region_6.7 | all-reduce | flops 4096 | bytes 32768 | tf_op jit(solution)/shard_map/psum | solution.py:36
  110.2 9.9 %collective-permute-start.2 = (bf16[2,4,1,128]{3,1,2,0:T(4,128)(2,1)S(1)}, bf16[2,4,1,128]{3,1,2,0:T(4,128)(2,1)S(1)}, u32[]{:S(2)}, u32[]{:S(2)}) collective-permute-start(bf16[2,4,1,128]{3,1,2,0:T(4,128)(2,1)S(1)} %get-tuple-element.40), channel_id=1, source_target_pairs={{0,1},{1,2},{2,3},{3,4},{4,5},{5,6},{6,7},{7,8},{8,9},{9,10},{10,1... | collective-permute-start | bytes 6152 | tf_op jit(solution)/shard_map/ppermute | solution.py:20
  120.9 1.9 collective-permute-start.3
  123.2 2.6 collective-permute-done.3
  129.4 16.2 %all-gather.11 = f32[16,2,32]{2,1,0:T(2,128)S(1)} all-gather(f32[1,2,32]{2,1,0:T(2,128)S(1)} %bitcast.587), channel_id=3, replica_groups=mesh['segment'=8,'patch'=16] {'patch'}, dimensions={0}, use_global_device_ids=true | all-gather | bytes 4352 | tf_op jit(solution)/shard_map/all_gather | solution.py:50
  146.4 27.2 %psum.86 = f32[2,32]{1,0:T(2,128)S(1)} all-reduce(f32[2,32]{1,0:T(2,128)S(1)} %reduce_sum.341), channel_id=1, replica_groups=mesh['segment'=8,'patch'=16] {'patch'}, use_global_device_ids=true, to_apply=%region_12.13 | all-reduce | flops 64 | bytes 512 | tf_op jit(solution)/shard_map/psum | solution.py:52
  174.4 1.9 collective-permute-start.5
  176.4 2.4 collective-permute-start.6
  180.4 2.6 collective-permute-done.6
  196.4 16.2 %all-gather.12 = f32[16,2,32]{2,1,0:T(2,128)S(1)} all-gather(f32[1,2,32]{2,1,0:T(2,128)S(1)} %bitcast.588), channel_id=4, replica_groups=mesh['segment'=8,'patch'=16] {'patch'}, dimensions={0}, use_global_device_ids=true | all-gather | bytes 4352 | tf_op jit(solution)/shard_map/all_gather | solution.py:50
  213.4 26.7 %psum.87 = f32[2,32]{1,0:T(2,128)S(1)} all-reduce(f32[2,32]{1,0:T(2,128)S(1)} %reduce_sum.354), channel_id=1, replica_groups=mesh['segment'=8,'patch'=16] {'patch'}, use_global_device_ids=true, to_apply=%region_18.19 | all-reduce | flops 64 | bytes 512 | tf_op jit(solution)/shard_map/psum | solution.py:52
  241.0 1.9 collective-permute-start.7
  242.9 2.6 collective-permute-start.8
  247.0 2.6 collective-permute-done.8
  263.1 16.2 %all-gather.13 = f32[16,2,32]{2,1,0:T(2,128)S(1)} all-gather(f32[1,2,32]{2,1,0:T(2,128)S(1)} %bitcast.589), channel_id=5, replica_groups=mesh['segment'=8,'patch'=16] {'patch'}, dimensions={0}, use_global_device_ids=true | all-gather | bytes 4352 | tf_op jit(solution)/shard_map/all_gather | solution.py:50
  280.1 26.7 %psum.88 = f32[2,32]{1,0:T(2,128)S(1)} all-reduce(f32[2,32]{1,0:T(2,128)S(1)} %reduce_sum.364), channel_id=1, replica_groups=mesh['segment'=8,'patch'=16] {'patch'}, use_global_device_ids=true, to_apply=%region_24.25 | all-reduce | flops 64 | bytes 512 | tf_op jit(solution)/shard_map/psum | solution.py:52
  307.7 1.9 collective-permute-start.9
  309.7 2.4 collective-permute-start.10
  313.7 2.6 collective-permute-done.10
  329.7 16.2 %all-gather.14 = f32[16,2,32]{2,1,0:T(2,128)S(1)} all-gather(f32[1,2,32]{2,1,0:T(2,128)S(1)} %bitcast.590), channel_id=6, replica_groups=mesh['segment'=8,'patch'=16] {'patch'}, dimensions={0}, use_global_device_ids=true | all-gather | bytes 4352 | tf_op jit(solution)/shard_map/all_gather | solution.py:50
  346.7 26.9 %psum.89 = f32[2,32]{1,0:T(2,128)S(1)} all-reduce(f32[2,32]{1,0:T(2,128)S(1)} %reduce_sum.444), channel_id=1, replica_groups=mesh['segment'=8,'patch'=16] {'patch'}, use_global_device_ids=true, to_apply=%region_30.31 | all-reduce | flops 64 | bytes 512 | tf_op jit(solution)/shard_map/psum | solution.py:52
  374.5 1.9 collective-permute-start.11
  376.4 2.4 collective-permute-start.12
  380.4 2.6 collective-permute-done.12
  394.6 2.0 convert_reduce_fusion.4
  396.7 16.2 %all-gather.15 = f32[16,2,32]{2,1,0:T(2,128)S(1)} all-gather(f32[1,2,32]{2,1,0:T(2,128)S(1)} %bitcast.591), channel_id=7, replica_groups=mesh['segment'=8,'patch'=16] {'patch'}, dimensions={0}, use_global_device_ids=true | all-gather | bytes 4352 | tf_op jit(solution)/shard_map/all_gather | solution.py:50
  413.2 1.9 collective-permute-start.17
  415.7 27.3 %psum.90 = f32[2,32]{1,0:T(2,128)S(1)} all-reduce(f32[2,32]{1,0:T(2,128)S(1)} %reduce_sum.451), channel_id=1, replica_groups=mesh['segment'=8,'patch'=16] {'patch'}, use_global_device_ids=true, to_apply=%region_36.37 | all-reduce | flops 64 | bytes 512 | tf_op jit(solution)/shard_map/psum | solution.py:52
  443.8 1.9 collective-permute-start.13
  445.7 2.4 collective-permute-start.14
  449.7 2.6 collective-permute-done.14
  455.5 34.4 %psum.91 = f32[2,4,4,128]{3,1,2,0:T(4,128)S(1)} all-reduce(f32[2,4,4,128]{3,1,2,0:T(4,128)S(1)} %fusion.107), channel_id=1, replica_groups=mesh['segment'=8,'patch'=16] {'segment'}, use_global_device_ids=true, to_apply=%region_37.38 | all-reduce | flops 4096 | bytes 32768 | tf_op jit(solution)/shard_map/psum | solution.py:36
  490.0 9.5 %collective-permute-start.15 = (bf16[2,4,1,128]{3,1,2,0:T(4,128)(2,1)S(1)}, bf16[2,4,1,128]{3,1,2,0:T(4,128)(2,1)S(1)}, u32[]{:S(2)}, u32[]{:S(2)}) collective-permute-start(bf16[2,4,1,128]{3,1,2,0:T(4,128)(2,1)S(1)} %get-tuple-element.38), channel_id=1, source_target_pairs={{0,1},{1,2},{2,3},{3,4},{4,5},{5,6},{6,7},{7,8},{8,9},{9,10},{10,1... | collective-permute-start | bytes 6152 | tf_op jit(solution)/shard_map/ppermute | solution.py:20
  499.5 2.3 collective-permute-start.16
  508.0 16.4 %all-gather.16 = f32[16,2,32]{2,1,0:T(2,128)S(1)} all-gather(f32[1,2,32]{2,1,0:T(2,128)S(1)} %bitcast.592), channel_id=8, replica_groups=mesh['segment'=8,'patch'=16] {'patch'}, dimensions={0}, use_global_device_ids=true | all-gather | bytes 4352 | tf_op jit(solution)/shard_map/all_gather | solution.py:50
  525.1 26.7 %psum.92 = f32[2,32]{1,0:T(2,128)S(1)} all-reduce(f32[2,32]{1,0:T(2,128)S(1)} %reduce_sum.458), channel_id=1, replica_groups=mesh['segment'=8,'patch'=16] {'patch'}, use_global_device_ids=true, to_apply=%region_43.44 | all-reduce | flops 64 | bytes 512 | tf_op jit(solution)/shard_map/psum | solution.py:52
  552.7 1.9 collective-permute-start.18
  554.6 2.4 collective-permute-start.19
  558.6 2.6 collective-permute-done.19
  574.7 16.2 %all-gather.17 = f32[16,2,32]{2,1,0:T(2,128)S(1)} all-gather(f32[1,2,32]{2,1,0:T(2,128)S(1)} %bitcast.593), channel_id=9, replica_groups=mesh['segment'=8,'patch'=16] {'patch'}, dimensions={0}, use_global_device_ids=true | all-gather | bytes 4352 | tf_op jit(solution)/shard_map/all_gather | solution.py:50
  591.7 26.7 %psum.93 = f32[2,32]{1,0:T(2,128)S(1)} all-reduce(f32[2,32]{1,0:T(2,128)S(1)} %reduce_sum.465), channel_id=1, replica_groups=mesh['segment'=8,'patch'=16] {'patch'}, use_global_device_ids=true, to_apply=%region_49.50 | all-reduce | flops 64 | bytes 512 | tf_op jit(solution)/shard_map/psum | solution.py:52
  619.2 1.9 collective-permute-start.20
  621.1 2.6 collective-permute-start.21
  625.2 2.6 collective-permute-done.21
  639.2 1.9 convert_reduce_fusion
  641.3 16.2 %all-gather.18 = f32[16,2,32]{2,1,0:T(2,128)S(1)} all-gather(f32[1,2,32]{2,1,0:T(2,128)S(1)} %bitcast.594), channel_id=10, replica_groups=mesh['segment'=8,'patch'=16] {'patch'}, dimensions={0}, use_global_device_ids=true | all-gather | bytes 4352 | tf_op jit(solution)/shard_map/all_gather | solution.py:50
  658.3 26.7 %psum.94 = f32[2,32]{1,0:T(2,128)S(1)} all-reduce(f32[2,32]{1,0:T(2,128)S(1)} %reduce_sum.472), channel_id=1, replica_groups=mesh['segment'=8,'patch'=16] {'patch'}, use_global_device_ids=true, to_apply=%region_55.56 | all-reduce | flops 64 | bytes 512 | tf_op jit(solution)/shard_map/psum | solution.py:52
  685.9 1.9 collective-permute-start.22
  687.8 2.4 collective-permute-start.23
  691.8 2.6 collective-permute-done.23
  707.9 16.2 %all-gather.19 = f32[16,2,32]{2,1,0:T(2,128)S(1)} all-gather(f32[1,2,32]{2,1,0:T(2,128)S(1)} %bitcast.595), channel_id=11, replica_groups=mesh['segment'=8,'patch'=16] {'patch'}, dimensions={0}, use_global_device_ids=true | all-gather | bytes 4352 | tf_op jit(solution)/shard_map/all_gather | solution.py:50
  724.8 26.9 %psum.95 = f32[2,32]{1,0:T(2,128)S(1)} all-reduce(f32[2,32]{1,0:T(2,128)S(1)} %reduce_sum.479), channel_id=1, replica_groups=mesh['segment'=8,'patch'=16] {'patch'}, use_global_device_ids=true, to_apply=%region_61.62 | all-reduce | flops 64 | bytes 512 | tf_op jit(solution)/shard_map/psum | solution.py:52
  752.6 1.9 collective-permute-start.24
  754.5 2.4 collective-permute-start.25
  758.5 2.6 collective-permute-done.25
  (300 shorter events, 151.7 us)
Async XLA Ops:
  0.6 58.5 %copy-start = (bf16[1,2,320,4,128]{4,3,2,1,0:T(4,128)(2,1)S(1)}, bf16[1,2,320,4,128]{4,3,2,1,0:T(4,128)(2,1)}, u32[]{:S(2)}) copy-start(bf16[1,2,320,4,128]{4,3,2,1,0:T(4,128)(2,1)} %param.12) | copy-start | bytes 1966084
  0.6 58.5 %copy-start.4 = (f32[320]{0:T(512)S(1)}, f32[320]{0:T(512)}, u32[]{:S(2)}) copy-start(f32[320]{0:T(512)} %param.22) | copy-start | bytes 3844
  0.7 58.5 %copy-start.3 = (f32[320]{0:T(512)S(1)}, f32[320]{0:T(512)}, u32[]{:S(2)}) copy-start(f32[320]{0:T(512)} %param.23) | copy-start | bytes 3844
  60.5 11.3 %collective-permute-start = (bf16[2,320,1,128]{3,1,2,0:T(8,128)(2,1)}, bf16[2,320,1,128]{3,1,2,0:T(8,128)(2,1)}, u32[]{:S(2)}, u32[]{:S(2)}) collective-permute-start(bf16[2,320,1,128]{3,1,2,0:T(8,128)(2,1)} %get-tuple-element.36), channel_id=1, source_target_pairs={{0,1},{1,2},{2,3},{3,4},{4,5},{5,6},{6,7},{7,8},{8,9},{9,10},{10,1... | collective-permute-start | bytes 491528 | tf_op jit(solution)/shard_map/ppermute | solution.py:20
  62.5 9.1 %copy-start.8 = (bf16[9,4,320]{2,1,0:T(4,128)(2,1)S(1)}, bf16[9,4,320]{2,1,0:T(4,128)(2,1)}, u32[]{:S(2)}) copy-start(bf16[9,4,320]{2,1,0:T(4,128)(2,1)} %param.21) | copy-start | bytes 69124
  62.5 9.3 %collective-permute-start.1 = (bf16[2,320,1,128]{3,1,2,0:T(8,128)(2,1)}, bf16[2,320,1,128]{3,1,2,0:T(8,128)(2,1)S(1)}, u32[]{:S(2)}, u32[]{:S(2)}) collective-permute-start(bf16[2,320,1,128]{3,1,2,0:T(8,128)(2,1)} %get-tuple-element.37), channel_id=1, source_target_pairs={{1,0},{2,1},{3,2},{4,3},{5,4},{6,5},{7,6},{8,7},{9,8},{10,9},{11,1... | collective-permute-start | bytes 491528 | tf_op jit(solution)/shard_map/ppermute | solution.py:23
  65.7 6.0 copy-start.7
  65.7 62.8 %collective-permute-start.4 = (bf16[2,320,4,128]{3,1,2,0:T(8,128)(2,1)S(1)}, bf16[2,320,4,128]{3,1,2,0:T(8,128)(2,1)S(1)}, u32[]{:S(2)}, u32[]{:S(2)}) collective-permute-start(bf16[2,320,4,128]{3,1,2,0:T(8,128)(2,1)S(1)} %bitcast.585), channel_id=1, source_target_pairs={{0,16},{16,32},{32,48},{48,64},{64,80},{80,96},{96,112},{1,17},{17... | collective-permute-start | bytes 1966088 | tf_op jit(solution)/shard_map/ppermute | solution.py:31
  76.2 34.0 %copy-start.2 = (f32[2,4,4,128]{3,2,1,0:T(4,128)S(1)}, f32[2,4,4,128]{3,2,1,0:T(4,128)}, u32[]{:S(2)}) copy-start(f32[2,4,4,128]{3,2,1,0:T(4,128)} %param.13) | copy-start | bytes 49156
  76.2 44.0 %copy-start.5 = (f32[1,2,2,320]{3,2,1,0:T(2,128)S(1)}, f32[1,2,2,320]{3,2,1,0:T(2,128)}, u32[]{:S(2)}) copy-start(f32[1,2,2,320]{3,2,1,0:T(2,128)} %param.19) | copy-start | bytes 15364
  76.2 44.0 %copy-start.6 = (f32[1,2,2,320]{3,2,1,0:T(2,128)S(1)}, f32[1,2,2,320]{3,2,1,0:T(2,128)}, u32[]{:S(2)}) copy-start(f32[1,2,2,320]{3,2,1,0:T(2,128)} %param.18) | copy-start | bytes 15364
  76.2 46.6 %copy-start.1 = (bf16[9,320,4]{1,2,0:T(4,128)(2,1)S(1)}, bf16[9,320,4]{1,2,0:T(4,128)(2,1)}, u32[]{:S(2)}) copy-start(bf16[9,320,4]{1,2,0:T(4,128)(2,1)} %param.20) | copy-start | bytes 69124
  110.2 12.6 %collective-permute-start.2 = (bf16[2,4,1,128]{3,1,2,0:T(4,128)(2,1)S(1)}, bf16[2,4,1,128]{3,1,2,0:T(4,128)(2,1)S(1)}, u32[]{:S(2)}, u32[]{:S(2)}) collective-permute-start(bf16[2,4,1,128]{3,1,2,0:T(4,128)(2,1)S(1)} %get-tuple-element.40), channel_id=1, source_target_pairs={{0,1},{1,2},{2,3},{3,4},{4,5},{5,6},{6,7},{7,8},{8,9},{9,10},{10,1... | collective-permute-start | bytes 6152 | tf_op jit(solution)/shard_map/ppermute | solution.py:20
  120.9 4.9 collective-permute-start.3
  174.4 5.9 collective-permute-start.5
  176.4 6.6 collective-permute-start.6
  241.0 6.0 collective-permute-start.7
  242.9 6.6 collective-permute-start.8
  307.7 5.9 collective-permute-start.9
  309.7 6.6 collective-permute-start.10
  374.5 5.9 collective-permute-start.11
  376.4 6.6 collective-permute-start.12
  413.2 94.0 %collective-permute-start.17 = (bf16[2,320,4,128]{3,1,2,0:T(8,128)(2,1)S(1)}, bf16[2,320,4,128]{3,1,2,0:T(8,128)(2,1)S(1)}, u32[]{:S(2)}, u32[]{:S(2)}) collective-permute-start(bf16[2,320,4,128]{3,1,2,0:T(8,128)(2,1)S(1)} %get-tuple-element.55), channel_id=1, source_target_pairs={{0,16},{16,32},{32,48},{48,64},{64,80},{80,96},{96,112},{1,17},{17... | collective-permute-start | bytes 1966088 | tf_op jit(solution)/shard_map/ppermute | solution.py:31
  443.8 5.9 collective-permute-start.13
  445.7 6.6 collective-permute-start.14
  490.0 12.5 %collective-permute-start.15 = (bf16[2,4,1,128]{3,1,2,0:T(4,128)(2,1)S(1)}, bf16[2,4,1,128]{3,1,2,0:T(4,128)(2,1)S(1)}, u32[]{:S(2)}, u32[]{:S(2)}) collective-permute-start(bf16[2,4,1,128]{3,1,2,0:T(4,128)(2,1)S(1)} %get-tuple-element.38), channel_id=1, source_target_pairs={{0,1},{1,2},{2,3},{3,4},{4,5},{5,6},{6,7},{7,8},{8,9},{9,10},{10,1... | collective-permute-start | bytes 6152 | tf_op jit(solution)/shard_map/ppermute | solution.py:20
  499.5 4.9 collective-permute-start.16
  552.7 5.9 collective-permute-start.18
  554.6 6.6 collective-permute-start.19
  619.2 6.0 collective-permute-start.20
  621.1 6.6 collective-permute-start.21
  685.9 5.9 collective-permute-start.22
  687.8 6.6 collective-permute-start.23
  752.6 5.9 collective-permute-start.24
  754.5 6.6 collective-permute-start.25
